TPU v7x, 32 devices: a whole 2x2x4 slice. The times are simulated.
32 devices in a mesh: virt: 8 (over y, x, core), occ: 4 (over z).
Axes of the slice: x: 2, y: 2, z: 4, core: 2. Of those that a mesh axis runs over, the one named last changes fastest.
Arguments:
- amplitudes: bfloat16 [512, 4096], P('occ', 'virt'), may hold values from -6 to 6
- integrals: bfloat16 [1024, 16384], P(None, 'virt'), may hold values from -0.1875 to 0.1875
- panel_owner: int32 [4, 2], P('occ'), may hold values from 0 to 7, as said below
- inter: bfloat16 [8192, 8192], P('occ', 'virt'), may hold values from -0.125 to 0.125
- dest: int32 [4, 8, 16], P('occ', 'virt'), may hold values from 0 to 3, as said below
- screen: int32 [4, 8, 16], P('occ', 'virt'), may hold values from 0 to 1
Outputs:
- contracted: bfloat16 [512, 8192], P('occ', 'virt')
Inputs may be any that keep to these rules, and one draw needn't show every extreme that they name: `panel_owner`: in each row the 2 entries are distinct. `dest`: among the subtiles of one device that screen marks 1, no two name the same owner.
All inputs are finite; a program needn't handle non-finite values.
Results may differ from a plain program's by a relative error of at most 0.0055.
Values may be sent and summed in bfloat16 or wider, within the bound.
A program may use at most 64 MiB of HBM per device.

v0:
```python
import jax
import jax.numpy as jnp
from jax import lax
from jax.sharding import PartitionSpec as P

SROWS = 32


def on_device(amplitudes, integrals, panel_owner, inter, dest, screen):
    op_rows = amplitudes.shape[0]
    tile = amplitudes.shape[1]
    cols = integrals.shape[1]
    steps = panel_owner.shape[1]
    n_sub = dest.shape[2]
    n_occ = lax.axis_size("occ")
    half_splits = op_rows // SROWS
    col_tiles = cols // tile
    every = lax.all_gather(amplitudes[None], "virt", axis=0, tiled=True)
    chosen_entries = jnp.take(every, panel_owner[0], axis=0)
    chosen_entries = chosen_entries.transpose(1, 0, 2).reshape(op_rows, steps * tile)
    accum = jnp.dot(chosen_entries, integrals, preferred_element_type=jnp.float32)
    ladder = accum.astype(jnp.bfloat16)
    subtiles = (
        ladder.reshape(half_splits, SROWS, col_tiles, tile)
        .transpose(0, 2, 1, 3)
        .reshape(n_sub, SROWS, tile)
    )
    owners = jnp.arange(n_occ, dtype=jnp.int32)
    labels = jnp.arange(1, n_sub + 1, dtype=jnp.int32)
    routing = (dest[0, 0][None, :] == owners[:, None]) & (screen[0, 0][None, :] == 1)
    outgoing = jnp.einsum(
        "os,srt->ort", routing.astype(jnp.bfloat16), subtiles, preferred_element_type=jnp.float32
    ).astype(jnp.bfloat16)
    output_marker = jnp.sum(routing.astype(jnp.int32) * labels[None, :], axis=1).astype(
        jnp.bfloat16
    )[:, None]
    arriving_tiles, tag_in = (
        lax.all_to_all(outgoing, "occ", split_axis=0, concat_axis=0, tiled=True),
        lax.all_to_all(output_marker, "occ", split_axis=0, concat_axis=0, tiled=True),
    )
    choose_surviving = tag_in.astype(jnp.float32) == labels[None, :].astype(jnp.float32)
    summed = jnp.einsum(
        "ez,ead->zad",
        choose_surviving.astype(jnp.bfloat16),
        arriving_tiles,
        preferred_element_type=jnp.float32,
    )
    gathered = summed.astype(jnp.bfloat16)
    left = (
        gathered.reshape(half_splits, col_tiles, SROWS, tile)
        .transpose(0, 2, 1, 3)
        .reshape(op_rows, cols)
    )
    return jnp.dot(left, inter, preferred_element_type=jnp.float32).astype(jnp.bfloat16)


def solution(mesh):
    return jax.shard_map(
        on_device,
        mesh=mesh,
        in_specs=(
            P("occ", "virt"),
            P(None, "virt"),
            P("occ", None),
            P("occ", "virt"),
            P("occ", "virt", None),
            P("occ", "virt", None),
        ),
        out_specs=P("occ", "virt"),
        check_vma=False,
    )
```

profile of v0, /device:TPU:0, one launch (start us, length us, event | category | flops | bytes accessed | tf_op | source)
XLA Modules:
  0.0 64.2 jit_solution(17440745688563391463)
XLA Ops:
  6.5 0.0 all-gather.3.cloned.1.call-start
  6.5 0.7 %all-gather.3.cloned.1.call-update = ((bf16[128,512]{1,0:T(8,128)(2,1)}), bf16[1024,512]{1,0:T(8,128)(2,1)}) async-update(((), (), s32[]{:S(2)}) %all-gather.3.cloned.1.call-start, bf16[128,512]{1,0:T(8,128)(2,1)} %param.6) | async-update | bytes 1310744
  7.3 0.7 %compare_bitcast_fusion = pred[16]{0:T(512)(128)(4,1)S(1)} fusion(s32[1,1,16]{2,1,0:T(1,128)} %param.11), kind=kLoop, calls=%fused_computation.19 | loop fusion | flops 16 | bytes 80 | tf_op jit(solution)/shard_map/eq | solution.py:30
  7.9 0.8 %select_reduce_fusion = s32[4]{0:T(128)S(1)} fusion(s32[16]{0:T(128)S(1)} %iota_add_fusion, s32[16]{0:T(128)} %bitcast.39, pred[16]{0:T(512)(128)(4,1)S(1)} %compare_bitcast_fusion), kind=kLoop, calls=%fused_computation.12 | loop fusion | flops 252 | bytes 160 | tf_op jit(solution)/shard_map/reduce_sum | solution.py:34
  8.7 0.7 %copy.20 = bf16[4,1,1]{2,1,0:T(2,128)(2,1)} copy(bf16[4,1,1]{0,2,1:T(2,128)(2,1)S(1)} %convert_bitcast_fusion) | data formatting | bytes 16 | tf_op jit(solution)/shard_map/convert_element_type | solution.py:34
  9.4 6.3 %all-to-all-start = ((bf16[4,1,1]{2,1,0:T(2,128)(2,1)}), bf16[4,1,1]{2,1,0:T(2,128)(2,1)S(1)}, u32[]{:S(2)}, u32[]{:S(2)}) async-start(bf16[4,1,1]{2,1,0:T(2,128)(2,1)} %copy.20), calls=%async_computation | async-start | bytes 4096 | tf_op jit(solution)/shard_map/all_to_all | solution.py:39
  15.7 0.7 %fusion.11 = s32[2]{0:T(128)S(1)} fusion(s32[1,2]{1,0:T(1,128)} %param.8), kind=kLoop, calls=%fused_computation.24 | loop fusion | flops 6 | bytes 16 | tf_op jit(solution)/shard_map/jit(_take)/jit(_where)/select_n | solution.py:19
  16.4 0.7 %compare_and_fusion = pred[2]{0:T(512)(128)(4,1)S(1)} fusion(s32[1,2]{1,0:T(1,128)} %param.8), kind=kLoop, calls=%fused_computation.17 | loop fusion | flops 12 | bytes 10 | tf_op jit(solution)/shard_map/jit(_take)/and | solution.py:19
  17.1 18.3 %all-gather.3.cloned.1.call-done = bf16[1024,512]{1,0:T(8,128)(2,1)} async-done(((bf16[128,512]{1,0:T(8,128)(2,1)}), bf16[1024,512]{1,0:T(8,128)(2,1)}) %all-gather.3.cloned.1.call-update) | async-done | bytes 1048592 | tf_op jit(solution)/shard_map/all_gather | solution.py:18
  35.3 1.8 %gather_fusion = bf16[2,128,512]{2,1,0:T(8,128)(2,1)S(1)} fusion(bf16[8,128,512]{2,1,0:T(8,128)(2,1)} %bitcast.38, s32[1024]{0:T(1024)S(1)} %pad_clamp_fusion), kind=kCustom, calls=%fused_computation | custom fusion | bytes 524296 | tf_op jit(solution)/shard_map/jit(_take)/gather | solution.py:19
  37.1 0.0 copy-start
  37.2 0.1 select_bitcast_fusion
  37.2 0.2 copy.21
  37.4 2.9 %convolution_convert_fusion = bf16[128,2048]{1,0:T(8,128)(2,1)S(1)} fusion(bf16[128,1024]{0,1:T(8,128)(2,1)S(1)} %bitcast.37, bf16[1024,2048]{1,0:T(8,128)(2,1)} %param.7), kind=kOutput, calls=%fused_computation.1 | convolution fusion | flops 537133056 | bytes 4980736 | tf_op jit(solution)/shard_map/dot_general | solution.py:21
  40.4 0.4 reshape.88
  40.7 0.1 copy.22
  40.9 0.0 copy-done
  40.9 0.4 convolution_convert_fusion.3
  41.3 0.7 %copy.24 = bf16[4,32,512]{2,1,0:T(8,128)(2,1)} copy(bf16[4,32,512]{2,0,1:T(4,128)(2,1)S(1)} %convolution_convert_fusion.3) | data formatting | bytes 262144 | tf_op jit(solution)/shard_map/convert_element_type | solution.py:33
  41.9 0.0 all-to-all-done
  41.9 4.6 %all-to-all-start.1 = ((bf16[4,32,512]{2,1,0:T(8,128)(2,1)}), bf16[4,32,512]{2,1,0:T(8,128)(2,1)S(1)}, u32[]{:S(2)}, u32[]{:S(2)}) async-start(bf16[4,32,512]{2,1,0:T(8,128)(2,1)} %copy.24), calls=%async_computation.1 | async-start | bytes 262144 | tf_op jit(solution)/shard_map/all_to_all | solution.py:38
  46.6 0.1 convert_reduce_fusion
  46.7 6.2 %all-to-all-done.1 = bf16[4,32,512]{2,1,0:T(8,128)(2,1)S(1)} async-done(((bf16[4,32,512]{2,1,0:T(8,128)(2,1)}), bf16[4,32,512]{2,1,0:T(8,128)(2,1)S(1)}, u32[]{:S(2)}, u32[]{:S(2)}) %all-to-all-start.1) | async-done | bytes 131104 | tf_op jit(solution)/shard_map/all_to_all | solution.py:38
  52.8 0.5 convolution_convert_fusion.1
  53.3 0.1 reshape.90
  53.4 0.2 copy.26
  53.6 0.1 copy.27
  53.7 3.7 %convolution_convert_fusion.2 = bf16[128,1024]{1,0:T(8,128)(2,1)} fusion(bf16[128,2048]{1,0:T(8,128)(2,1)S(1)} %bitcast.34, bf16[2048,1024]{1,0:T(8,128)(2,1)} %param.9), kind=kOutput, calls=%fused_computation.3 | convolution fusion | flops 537001984 | bytes 4980736 | tf_op jit(solution)/shard_map/dot_general | solution.py:54
  (4 shorter events, 0.0 us)
Async XLA Ops:
  6.5 28.8 %all-gather.3.cloned.1.call-start = ((), (), s32[]{:S(2)}) async-start(), calls=%async_computation.2 | async-start | bytes 1179648 | tf_op jit(solution)/shard_map/all_gather | solution.py:18
  9.4 32.5 %all-to-all-start = ((bf16[4,1,1]{2,1,0:T(2,128)(2,1)}), bf16[4,1,1]{2,1,0:T(2,128)(2,1)S(1)}, u32[]{:S(2)}, u32[]{:S(2)}) async-start(bf16[4,1,1]{2,1,0:T(2,128)(2,1)} %copy.20), calls=%async_computation | async-start | bytes 4096 | tf_op jit(solution)/shard_map/all_to_all | solution.py:39
  37.1 3.7 %copy-start = (s32[1,1,16]{2,1,0:T(1,128)S(1)}, s32[1,1,16]{2,1,0:T(1,128)}, u32[]{:S(2)}) copy-start(s32[1,1,16]{2,1,0:T(1,128)} %param.10) | copy-start | bytes 196
  41.9 10.9 %all-to-all-start.1 = ((bf16[4,32,512]{2,1,0:T(8,128)(2,1)}), bf16[4,32,512]{2,1,0:T(8,128)(2,1)S(1)}, u32[]{:S(2)}, u32[]{:S(2)}) async-start(bf16[4,32,512]{2,1,0:T(8,128)(2,1)} %copy.24), calls=%async_computation.1 | async-start | bytes 262144 | tf_op jit(solution)/shard_map/all_to_all | solution.py:38
Sparse Core Ops, SparseCore 0:
  9.2 26.0 all-gather.2
where the time goes:
time: 64.6 us; the launch traced here: 64.2 us
  waiting for transfers between devices  25.2 us (39%)
  between operations  13.5 us (21%)
  starting transfers between devices  11 us (17%)
  matrix products  7.44 us (12%)
  local copies, waits for them, and re-layouts  4.21 us (7%)
  other arithmetic  2.98 us (5%)
    all_gather x1, waiting for transfers between devices, on_device(): every = lax.all_gather(amplitudes[None], 'virt', axis=0, tiled=True)  18.3 us
    all_to_all x1, starting transfers between devices, on_device(): lax.all_to_all(output_marker, 'occ', split_axis=0, concat_axis=0, tiled=T...  6.35 us
    all_to_all x1, waiting for transfers between devices, on_device(): lax.all_to_all(outgoing, 'occ', split_axis=0, concat_axis=0, tiled=True)  6.18 us
    all_to_all x1, starting transfers between devices, on_device(): lax.all_to_all(outgoing, 'occ', split_axis=0, concat_axis=0, tiled=True)  4.6 us
    dot_general x1, matrix products, on_device(): jnp.dot(left, inter, preferred_element_type=jnp.float32)  3.65 us
    dot_general x1, matrix products, on_device(): jnp.dot(chosen_entries, integrals, preferred_element_type=jnp.float32)  2.93 us
    gather x1, local copies, waits for them, and re-layouts, on_device(): chosen_entries = jnp.take(every, panel_owner[0], axis=0)  1.79 us
  transfers between devices with their start and end apart: 3, of which 2 were waited for; matrix products, arithmetic and copies ran while one was open for 16% of the time, Pallas kernels for 0%

commit v1 on v0

--- a/solution.py
+++ b/solution.py
@@ -15,7 +15,9 @@
     n_occ = lax.axis_size("occ")
     half_splits = op_rows // SROWS
     col_tiles = cols // tile
-    every = lax.all_gather(amplitudes[None], "virt", axis=0, tiled=True)
+    every = jnp.concatenate(
+        lax.all_to_all(jnp.stack([amplitudes[None]] * lax.axis_size("virt")), "virt", 0, 0), axis=0
+    )
     chosen_entries = jnp.take(every, panel_owner[0], axis=0)
     chosen_entries = chosen_entries.transpose(1, 0, 2).reshape(op_rows, steps * tile)
     accum = jnp.dot(chosen_entries, integrals, preferred_element_type=jnp.float32)

time: 64.6 us -> 48.8 us (0.76)
  between operations: 13.5 us -> 0.09 us
  waiting for transfers between devices: 25.2 us -> 17.9 us
  starting transfers between devices: 11 us -> 15 us
  local copies, waits for them, and re-layouts: 4.21 us -> 4.94 us
    all_gather x1 -> x0, waiting for transfers between devices: 18.3 us -> none  [on_device(): every = lax.all_gather(amplitudes[None], 'virt', axis=0, tiled=True)]
    all_to_all x0 -> x1, waiting for transfers between devices: none -> 11.9 us  [on_device(): lax.all_to_all(jnp.stack([amplitudes[None]] * lax.axis_size('virt')), 'vi...]
    all_to_all x0 -> x1, starting transfers between devices: none -> 5.2 us  [on_device(): lax.all_to_all(jnp.stack([amplitudes[None]] * lax.axis_size('virt')), 'vi...]
    another operation x0 -> x1, local copies, waits for them, and re-layouts: none -> 1.97 us  [on_device(): jnp.stack([amplitudes[None]] * lax.axis_size('virt'))]
    all_to_all x1, starting transfers between devices: 6.35 us -> 4.87 us  [on_device(): lax.all_to_all(output_marker, 'occ', split_axis=0, concat_axis=0, tiled=T...]
    gather x1, local copies, waits for them, and re-layouts: 1.79 us -> 0.56 us  [on_device(): chosen_entries = jnp.take(every, panel_owner[0], axis=0)]
    unnamed x1 -> x0, waiting for transfers between devices: 0.71 us -> none
  transfers between devices with their start and end apart: 3 -> 3, of which waited for: 2 -> 3; matrix products, arithmetic and copies ran while one was open for 16% -> 18% of each run, Pallas kernels for 0% -> 0%
where the time goes in v1:
time: 48.8 us; the launch traced here: 48.4 us
  waiting for transfers between devices  17.9 us (37%)
  starting transfers between devices  15 us (31%)
  matrix products  7.44 us (15%)
  local copies, waits for them, and re-layouts  4.94 us (10%)
  other arithmetic  2.98 us (6%)
    all_to_all x1, waiting for transfers between devices, on_device(): lax.all_to_all(jnp.stack([amplitudes[None]] * lax.axis_size('virt')), 'vi...  11.9 us
    all_to_all x1, waiting for transfers between devices, on_device(): lax.all_to_all(outgoing, 'occ', split_axis=0, concat_axis=0, tiled=True)  5.8 us
    all_to_all x1, starting transfers between devices, on_device(): lax.all_to_all(jnp.stack([amplitudes[None]] * lax.axis_size('virt')), 'vi...  5.2 us
    all_to_all x1, starting transfers between devices, on_device(): lax.all_to_all(outgoing, 'occ', split_axis=0, concat_axis=0, tiled=True)  4.89 us
    all_to_all x1, starting transfers between devices, on_device(): lax.all_to_all(output_marker, 'occ', split_axis=0, concat_axis=0, tiled=T...  4.87 us
    dot_general x1, matrix products, on_device(): jnp.dot(left, inter, preferred_element_type=jnp.float32)  3.65 us
    dot_general x1, matrix products, on_device(): jnp.dot(chosen_entries, integrals, preferred_element_type=jnp.float32)  2.93 us
    another operation x1, local copies, waits for them, and re-layouts, on_device(): jnp.stack([amplitudes[None]] * lax.axis_size('virt'))  1.97 us
  transfers between devices with their start and end apart: 3, of which 3 were waited for; matrix products, arithmetic and copies ran while one was open for 18% of the time, Pallas kernels for 0%

profile of v1, /device:TPU:0, one launch (start us, length us, event | category | flops | bytes accessed | tf_op | source)
XLA Modules:
  0.0 48.4 jit_solution(9759538396323521073)
XLA Ops:
  0.0 2.0 %stack.3 = bf16[8,1,128,512]{3,2,1,0:T(8,128)(2,1)} broadcast(bf16[128,512]{1,0:T(8,128)(2,1)} %param.6), dimensions={2,3} | broadcast | bytes 1179648 | tf_op jit(solution)/shard_map/stack | solution.py:19
  2.0 5.2 %all-to-all-start.1 = ((bf16[8,1,128,512]{3,2,1,0:T(8,128)(2,1)}), bf16[8,1,128,512]{3,2,1,0:T(8,128)(2,1)S(1)}, u32[]{:S(2)}, u32[]{:S(2)}) async-start(bf16[8,1,128,512]{3,2,1,0:T(8,128)(2,1)} %stack.3), calls=%async_computation.1 | async-start | bytes 2097152 | tf_op jit(solution)/shard_map/all_to_all | solution.py:19
  7.2 0.7 %compare_bitcast_fusion = pred[16]{0:T(512)(128)(4,1)S(1)} fusion(s32[1,1,16]{2,1,0:T(1,128)} %param.11), kind=kLoop, calls=%fused_computation.19 | loop fusion | flops 16 | bytes 80 | tf_op jit(solution)/shard_map/eq | solution.py:32
  7.8 0.8 %select_reduce_fusion = s32[4]{0:T(128)S(1)} fusion(s32[16]{0:T(128)S(1)} %iota_add_fusion, s32[16]{0:T(128)} %bitcast.39, pred[16]{0:T(512)(128)(4,1)S(1)} %compare_bitcast_fusion), kind=kLoop, calls=%fused_computation.12 | loop fusion | flops 252 | bytes 160 | tf_op jit(solution)/shard_map/reduce_sum | solution.py:36
  8.6 0.7 %copy.20 = bf16[4,1,1]{2,1,0:T(2,128)(2,1)} copy(bf16[4,1,1]{0,2,1:T(2,128)(2,1)S(1)} %convert_bitcast_fusion) | data formatting | bytes 16 | tf_op jit(solution)/shard_map/convert_element_type | solution.py:36
  9.3 0.7 %fusion.11 = s32[2]{0:T(128)S(1)} fusion(s32[1,2]{1,0:T(1,128)} %param.8), kind=kLoop, calls=%fused_computation.24 | loop fusion | flops 6 | bytes 16 | tf_op jit(solution)/shard_map/jit(_take)/jit(_where)/select_n | solution.py:21
  10.0 0.7 %compare_and_fusion = pred[2]{0:T(512)(128)(4,1)S(1)} fusion(s32[1,2]{1,0:T(1,128)} %param.8), kind=kLoop, calls=%fused_computation.17 | loop fusion | flops 12 | bytes 10 | tf_op jit(solution)/shard_map/jit(_take)/and | solution.py:21
  10.6 11.9 %all-to-all-done.1 = bf16[8,1,128,512]{3,2,1,0:T(8,128)(2,1)S(1)} async-done(((bf16[8,1,128,512]{3,2,1,0:T(8,128)(2,1)}), bf16[8,1,128,512]{3,2,1,0:T(8,128)(2,1)S(1)}, u32[]{:S(2)}, u32[]{:S(2)}) %all-to-all-start.1) | async-done | bytes 1048608 | tf_op jit(solution)/shard_map/all_to_all | solution.py:19
  22.5 4.9 %all-to-all-start = ((bf16[4,1,1]{2,1,0:T(2,128)(2,1)}), bf16[4,1,1]{2,1,0:T(2,128)(2,1)S(1)}, u32[]{:S(2)}, u32[]{:S(2)}) async-start(bf16[4,1,1]{2,1,0:T(2,128)(2,1)} %copy.20), calls=%async_computation | async-start | bytes 4096 | tf_op jit(solution)/shard_map/all_to_all | solution.py:41
  27.4 0.6 %gather_fusion = bf16[2,128,512]{2,1,0:T(8,128)(2,1)S(1)} fusion(bf16[8,128,512]{2,1,0:T(8,128)(2,1)S(1)} %bitcast.37, s32[1024]{0:T(1024)S(1)} %pad_clamp_fusion), kind=kCustom, calls=%fused_computation | custom fusion | bytes 524296 | tf_op jit(solution)/shard_map/jit(_take)/gather | solution.py:21
  28.0 0.0 copy-start
  28.0 0.1 select_bitcast_fusion
  28.1 0.2 copy.21
  28.3 2.9 %convolution_convert_fusion = bf16[128,2048]{1,0:T(8,128)(2,1)S(1)} fusion(bf16[128,1024]{0,1:T(8,128)(2,1)S(1)} %bitcast.38, bf16[1024,2048]{1,0:T(8,128)(2,1)} %param.7), kind=kOutput, calls=%fused_computation.1 | convolution fusion | flops 537133056 | bytes 4980736 | tf_op jit(solution)/shard_map/dot_general | solution.py:23
  31.2 0.4 reshape.94
  31.6 0.1 copy.22
  31.7 0.0 copy-done
  31.7 0.4 convolution_convert_fusion.3
  32.1 0.7 %copy.24 = bf16[4,32,512]{2,1,0:T(8,128)(2,1)} copy(bf16[4,32,512]{2,0,1:T(4,128)(2,1)S(1)} %convolution_convert_fusion.3) | data formatting | bytes 262144 | tf_op jit(solution)/shard_map/convert_element_type | solution.py:35
  32.8 0.2 all-to-all-done
  33.0 4.9 %all-to-all-start.2 = ((bf16[4,32,512]{2,1,0:T(8,128)(2,1)}), bf16[4,32,512]{2,1,0:T(8,128)(2,1)S(1)}, u32[]{:S(2)}, u32[]{:S(2)}) async-start(bf16[4,32,512]{2,1,0:T(8,128)(2,1)} %copy.24), calls=%async_computation.2 | async-start | bytes 262144 | tf_op jit(solution)/shard_map/all_to_all | solution.py:40
  37.9 0.1 convert_reduce_fusion
  38.0 5.8 %all-to-all-done.2 = bf16[4,32,512]{2,1,0:T(8,128)(2,1)S(1)} async-done(((bf16[4,32,512]{2,1,0:T(8,128)(2,1)}), bf16[4,32,512]{2,1,0:T(8,128)(2,1)S(1)}, u32[]{:S(2)}, u32[]{:S(2)}) %all-to-all-start.2) | async-done | bytes 131104 | tf_op jit(solution)/shard_map/all_to_all | solution.py:40
  43.8 0.5 convolution_convert_fusion.1
  44.3 0.1 reshape.96
  44.4 0.2 copy.26
  44.6 0.1 copy.27
  44.7 3.7 %convolution_convert_fusion.2 = bf16[128,1024]{1,0:T(8,128)(2,1)} fusion(bf16[128,2048]{1,0:T(8,128)(2,1)S(1)} %bitcast.34, bf16[2048,1024]{1,0:T(8,128)(2,1)} %param.9), kind=kOutput, calls=%fused_computation.3 | convolution fusion | flops 537001984 | bytes 4980736 | tf_op jit(solution)/shard_map/dot_general | solution.py:56
  (4 shorter events, 0.0 us)
Async XLA Ops:
  2.0 20.6 %all-to-all-start.1 = ((bf16[8,1,128,512]{3,2,1,0:T(8,128)(2,1)}), bf16[8,1,128,512]{3,2,1,0:T(8,128)(2,1)S(1)}, u32[]{:S(2)}, u32[]{:S(2)}) async-start(bf16[8,1,128,512]{3,2,1,0:T(8,128)(2,1)} %stack.3), calls=%async_computation.1 | async-start | bytes 2097152 | tf_op jit(solution)/shard_map/all_to_all | solution.py:19
  22.5 10.4 %all-to-all-start = ((bf16[4,1,1]{2,1,0:T(2,128)(2,1)}), bf16[4,1,1]{2,1,0:T(2,128)(2,1)S(1)}, u32[]{:S(2)}, u32[]{:S(2)}) async-start(bf16[4,1,1]{2,1,0:T(2,128)(2,1)} %copy.20), calls=%async_computation | async-start | bytes 4096 | tf_op jit(solution)/shard_map/all_to_all | solution.py:41
  28.0 3.7 %copy-start = (s32[1,1,16]{2,1,0:T(1,128)S(1)}, s32[1,1,16]{2,1,0:T(1,128)}, u32[]{:S(2)}) copy-start(s32[1,1,16]{2,1,0:T(1,128)} %param.10) | copy-start | bytes 196
  33.0 10.8 %all-to-all-start.2 = ((bf16[4,32,512]{2,1,0:T(8,128)(2,1)}), bf16[4,32,512]{2,1,0:T(8,128)(2,1)S(1)}, u32[]{:S(2)}, u32[]{:S(2)}) async-start(bf16[4,32,512]{2,1,0:T(8,128)(2,1)} %copy.24), calls=%async_computation.2 | async-start | bytes 262144 | tf_op jit(solution)/shard_map/all_to_all | solution.py:40
